TPU v7x, 32 devices: a whole 2x2x4 slice. The times are simulated.
32 devices in a mesh: rep: 8 (over y, x, core), fsdp: 4 (over z).
Axes of the slice: x: 2, y: 2, z: 4, core: 2. Of those that a mesh axis runs over, the one named last changes fastest.
Arguments:
- inputs: bfloat16 [24576, 768], P(('rep', 'fsdp')), may hold values from -6 to 6
- first_values: bfloat16 [24576, 384], P(('rep', 'fsdp')), may hold values from -6 to 6
- cotangent: bfloat16 [24576, 768], P(('rep', 'fsdp')), may hold values from -6 to 6
- tree_ids: int32 [24576], P('rep'), may hold values from 0 to 2, as said below
- segment_ids: int32 [24576], P('rep'), may hold values from 0 to 12, as said below
- path_table: int32 [24, 13, 3], P('rep'), may hold values from 0 to 12, as said below
- attn_gain: bfloat16 [768], P('fsdp'), may hold values from 0.5 to 1.5
- attn_shift: bfloat16 [768], P('fsdp'), may hold values from -3 to 3
- w_query: bfloat16 [768, 768], P('fsdp'), may hold values from -0.21875 to 0.21875
- w_key: bfloat16 [768, 768], P('fsdp'), may hold values from -0.21875 to 0.21875
- w_value: bfloat16 [768, 384], P('fsdp'), may hold values from -0.21875 to 0.21875
- w_out: bfloat16 [768, 768], P('fsdp'), may hold values from -1.75 to 1.75
- mlp_gain: bfloat16 [768], P('fsdp'), may hold values from 0.5 to 1.5
- mlp_shift: bfloat16 [768], P('fsdp'), may hold values from -3 to 3
- w_in: bfloat16 [768, 3072], P('fsdp'), may hold values from -0.21875 to 0.21875
- w_down: bfloat16 [3072, 768], P('fsdp'), may hold values from -0.109375 to 0.109375
Outputs:
- outputs: bfloat16 [24576, 768], P(('rep', 'fsdp'))
- input_grad: float32 [24576, 768], P(('rep', 'fsdp'))
- first_values_grad: float32 [24576, 384], P(('rep', 'fsdp'))
- attn_gain_grad: float32 [768], P('fsdp')
- attn_shift_grad: float32 [768], P('fsdp')
- w_query_grad: float32 [768, 768], P('fsdp')
- w_key_grad: float32 [768, 768], P('fsdp')
- w_value_grad: float32 [768, 384], P('fsdp')
- w_out_grad: float32 [768, 768], P('fsdp')
- mlp_gain_grad: float32 [768], P('fsdp')
- mlp_shift_grad: float32 [768], P('fsdp')
- w_in_grad: float32 [768, 3072], P('fsdp')
- w_down_grad: float32 [3072, 768], P('fsdp')
Inputs may be any that keep to these rules, and one draw needn't show every extreme that they name: `tree_ids`: within each aligned block of 3072 tokens every tree number 0 to 2 covers exactly one aligned run of 1024 consecutive tokens. `segment_ids`: each tree's tokens are its trunk (segment 0, 512 tokens), then 4 branches of 64 tokens numbered 1 to 4 in some order, then 4 * 2 leaves of 32 tokens numbered 4 + 1 and up in some order. `path_table`: row t, s lists the trunk, the branch and the leaf on the path to segment s of tree t, repeating the segment itself where it is shallower; every branch is the parent of 2 leaves. Tree t of group r is row r * 3 + t.
All inputs are finite; a program needn't handle non-finite values.
Results may differ from a plain program's by a relative error of at most 0.013.
Values may be sent and summed in bfloat16 or wider, within the bound.
A program may use at most 192 MiB of HBM per device.

v0:
```python
import jax
import jax.numpy as jnp
from jax import lax
from jax.sharding import PartitionSpec as P

HEAD = 64
TREE_LEN = 1024
epsilon = 1e-05
far_below = -1e30


def shifted(block, axis, distance):
    devices = range(lax.axis_size(axis))
    route = [(i - distance, i) for i in devices if i - distance in devices]
    return lax.ppermute(block, axis, route)


def affine_norm(values_in, gain_vec, shift_vec):
    center = values_in - jnp.mean(values_in, axis=1, keepdims=True)
    spread = jnp.mean(center * center, axis=1, keepdims=True)
    return center * lax.rsqrt(spread + epsilon) * gain_vec + shift_vec


def gelu_tanh(values_in):
    return jax.nn.gelu(values_in, approximate=True)


def path_rows(tree_ids, segment_ids, path_table):
    seg_count = path_table.shape[1]
    flat_table = path_table.reshape(-1, 3)
    lookup = tree_ids * seg_count + segment_ids
    onehot = (lookup[:, None] == jnp.arange(flat_table.shape[0], dtype=jnp.int32)[None, :]).astype(
        jnp.int32
    )
    return jnp.sum(onehot[:, :, None] * flat_table[None, :, :], axis=1)


def visible_mask(tree_ids, segment_ids, path_table, row_start, row_count, key_start, window_len):
    paths = path_rows(tree_ids, segment_ids, path_table)
    query_tree = lax.dynamic_slice_in_dim(tree_ids, row_start, row_count, 0)
    query_path = lax.dynamic_slice_in_dim(paths, row_start, row_count, 0)
    query_pos = row_start + jnp.arange(row_count, dtype=jnp.int32)
    key_pos = key_start + jnp.arange(window_len, dtype=jnp.int32)
    inside = key_pos >= 0
    safe_pos = jnp.clip(key_pos, 0, tree_ids.shape[0] - 1)
    key_tree = jnp.take(tree_ids, safe_pos)
    key_seg = jnp.take(segment_ids, safe_pos)
    same_tree = query_tree[:, None] == key_tree[None, :]
    earlier = key_pos[None, :] <= query_pos[:, None]
    on_path = (
        (key_seg[None, :] == query_path[:, 0:1])
        | (key_seg[None, :] == query_path[:, 1:2])
        | (key_seg[None, :] == query_path[:, 2:3])
    )
    return inside[None, :] & same_tree & earlier & on_path


def pair_slice(block, pair_index):
    return lax.dynamic_slice_in_dim(block, pair_index * 2 * HEAD, 2 * HEAD, 1).reshape(
        block.shape[0], 2, HEAD
    )


def pair_scores(query_pair, key_pair, visible):
    scores = jnp.einsum(
        "qhd,khd->hqk", query_pair, key_pair, preferred_element_type=jnp.float32
    ) * HEAD ** (-0.5)
    return jnp.where(visible[None, :, :], scores, far_below)


def reorder_rows(grad_block, fsdp_count, rep_count):
    return grad_block.reshape(fsdp_count, rep_count, -1).transpose(1, 0, 2).reshape(-1)


def fetch_earlier(both_rows, distance):
    return shifted(both_rows, "fsdp", distance)


def return_earlier(grad_rows, distance):
    return shifted(grad_rows.astype(jnp.bfloat16), "fsdp", -distance).astype(grad_rows.dtype)


def on_device(
    inputs,
    first_values,
    cotangent,
    tree_ids,
    segment_ids,
    path_table,
    attn_gain,
    attn_shift,
    w_query,
    w_key,
    w_value,
    w_out,
    mlp_gain,
    mlp_shift,
    w_in,
    w_down,
):
    row_count, feat_width = inputs.shape
    scale = HEAD ** (-0.5)
    fsdp_count = lax.axis_size("fsdp")
    reach = 0
    for device_pos in range(fsdp_count):
        offset = device_pos * row_count % TREE_LEN
        reach = max(reach, (offset + row_count - 1) // row_count)
    window_len = (reach + 1) * row_count
    row_start = lax.axis_index("fsdp") * row_count
    gain1, shift1, query_w, key_w, value_w, out_w = (
        lax.all_gather(attn_gain, "fsdp", axis=0, tiled=True),
        lax.all_gather(attn_shift, "fsdp", axis=0, tiled=True),
        lax.all_gather(w_query, "fsdp", axis=0, tiled=True),
        lax.all_gather(w_key, "fsdp", axis=0, tiled=True),
        lax.all_gather(w_value, "fsdp", axis=0, tiled=True),
        lax.all_gather(w_out, "fsdp", axis=0, tiled=True),
    )
    resid_in = inputs.astype(jnp.float32)
    normed1_f, norm1_back = jax.vjp(
        affine_norm, resid_in, gain1.astype(jnp.float32), shift1.astype(jnp.float32)
    )
    normed1 = normed1_f.astype(jnp.bfloat16)
    queries = jnp.dot(normed1, query_w, preferred_element_type=jnp.float32).astype(jnp.bfloat16)
    key_rows = jnp.dot(normed1, key_w, preferred_element_type=jnp.float32).astype(jnp.bfloat16)
    fresh = jnp.dot(normed1, value_w, preferred_element_type=jnp.float32).astype(jnp.bfloat16)
    value_rows = jnp.concatenate([fresh, first_values], axis=1)
    both_rows = jnp.concatenate([key_rows, value_rows], axis=1)
    near_parts = []
    for distance in range(reach, 0, -1):
        near_parts.append(fetch_earlier(both_rows, distance))
    near_parts.append(both_rows)
    window_rows = jnp.concatenate(near_parts, axis=0)
    win_keys = window_rows[:, :feat_width]
    win_values = window_rows[:, feat_width:]
    key_start = row_start - reach * row_count
    visible = visible_mask(
        tree_ids, segment_ids, path_table, row_start, row_count, key_start, window_len
    )
    head_count = feat_width // HEAD
    pair_count = head_count // 2

    def forward_pair(pair_index, carry):
        mixed_acc, lse_acc = carry
        query_pair = pair_slice(queries, pair_index)
        key_pair = pair_slice(win_keys, pair_index)
        value_pair = pair_slice(win_values, pair_index)
        scores = pair_scores(query_pair, key_pair, visible)
        row_max = jnp.max(scores, axis=2, keepdims=True)
        expo = jnp.exp(scores - row_max)
        denom_sum = jnp.sum(expo, axis=2, keepdims=True)
        probs = expo / denom_sum
        lse_pair = (row_max + jnp.log(denom_sum))[:, :, 0]
        weights_b = probs.astype(jnp.bfloat16)
        pair_out = jnp.einsum(
            "hqk,khd->qhd", weights_b, value_pair, preferred_element_type=jnp.float32
        )
        pair_out = pair_out.reshape(row_count, 2 * HEAD).astype(jnp.bfloat16)
        mixed_acc = lax.dynamic_update_slice_in_dim(mixed_acc, pair_out, pair_index * 2 * HEAD, 1)
        lse_acc = lax.dynamic_update_slice_in_dim(lse_acc, lse_pair, pair_index * 2, 0)
        return (mixed_acc, lse_acc)

    mixed, lse_all = lax.fori_loop(
        0,
        pair_count,
        forward_pair,
        (
            jnp.zeros((row_count, feat_width), jnp.bfloat16),
            jnp.zeros((head_count, row_count), jnp.float32),
        ),
    )
    resid = resid_in + jnp.dot(mixed, out_w, preferred_element_type=jnp.float32)
    gain2, shift2, inner_w, down_w = (
        lax.all_gather(mlp_gain, "fsdp", axis=0, tiled=True),
        lax.all_gather(mlp_shift, "fsdp", axis=0, tiled=True),
        lax.all_gather(w_in, "fsdp", axis=0, tiled=True),
        lax.all_gather(w_down, "fsdp", axis=0, tiled=True),
    )
    normed2_f, norm2_back = jax.vjp(
        affine_norm, resid, gain2.astype(jnp.float32), shift2.astype(jnp.float32)
    )
    normed2 = normed2_f.astype(jnp.bfloat16)
    act = jnp.dot(normed2, inner_w, preferred_element_type=jnp.float32)
    hidden_f, gelu_back = jax.vjp(gelu_tanh, act)
    hidden = hidden_f.astype(jnp.bfloat16)
    outputs = (resid + jnp.dot(hidden, down_w, preferred_element_type=jnp.float32)).astype(
        jnp.bfloat16
    )
    grad_hidden = jnp.dot(cotangent, down_w.T, preferred_element_type=jnp.float32)
    down_grad = jnp.dot(hidden.T, cotangent, preferred_element_type=jnp.float32)
    grad_act = gelu_back(grad_hidden)[0].astype(jnp.bfloat16)
    inner_grad = jnp.dot(normed2.T, grad_act, preferred_element_type=jnp.float32)
    grad_normed2 = jnp.dot(grad_act, inner_w.T, preferred_element_type=jnp.float32)
    grad_ln2, gain2_grad, shift2_grad = norm2_back(grad_normed2)
    grad_resid = cotangent.astype(jnp.float32) + grad_ln2
    grad_branch = grad_resid.astype(jnp.bfloat16)
    out_grad = jnp.dot(mixed.T, grad_branch, preferred_element_type=jnp.float32)
    grad_mixed = jnp.dot(grad_branch, out_w.T, preferred_element_type=jnp.float32).astype(
        jnp.bfloat16
    )

    def backward_pair(pair_index, carry):
        query_acc, key_acc, value_acc = carry
        query_pair = pair_slice(queries, pair_index)
        key_pair = pair_slice(win_keys, pair_index)
        value_pair = pair_slice(win_values, pair_index)
        grad_pair = pair_slice(grad_mixed, pair_index)
        scores = pair_scores(query_pair, key_pair, visible)
        lse_pair = lax.dynamic_slice_in_dim(lse_all, pair_index * 2, 2, 0)
        probs = jnp.exp(scores - lse_pair[:, :, None])
        weights_b = probs.astype(jnp.bfloat16)
        grad_weights = jnp.einsum(
            "qhd,khd->hqk", grad_pair, value_pair, preferred_element_type=jnp.float32
        )
        inner_sum = jnp.sum(probs * grad_weights, axis=2, keepdims=True)
        grad_scores = (probs * (grad_weights - inner_sum)).astype(jnp.bfloat16)
        query_part = (
            jnp.einsum("hqk,khd->qhd", grad_scores, key_pair, preferred_element_type=jnp.float32)
            * scale
        )
        key_part = (
            jnp.einsum("hqk,qhd->khd", grad_scores, query_pair, preferred_element_type=jnp.float32)
            * scale
        )
        value_part = jnp.einsum(
            "hqk,qhd->khd", weights_b, grad_pair, preferred_element_type=jnp.float32
        )
        query_acc = lax.dynamic_update_slice_in_dim(
            query_acc, query_part.reshape(row_count, 2 * HEAD), pair_index * 2 * HEAD, 1
        )
        key_acc = lax.dynamic_update_slice_in_dim(
            key_acc, key_part.reshape(window_len, 2 * HEAD), pair_index * 2 * HEAD, 1
        )
        value_acc = lax.dynamic_update_slice_in_dim(
            value_acc, value_part.reshape(window_len, 2 * HEAD), pair_index * 2 * HEAD, 1
        )
        return (query_acc, key_acc, value_acc)

    query_full, key_win, value_win = lax.fori_loop(
        0,
        pair_count,
        backward_pair,
        (
            jnp.zeros((row_count, feat_width), jnp.float32),
            jnp.zeros((window_len, feat_width), jnp.float32),
            jnp.zeros((window_len, feat_width), jnp.float32),
        ),
    )
    grad_window = jnp.concatenate([key_win, value_win], axis=1).reshape(
        reach + 1, row_count, 2 * feat_width
    )
    own_grad = grad_window[reach]
    for distance in range(1, reach + 1):
        own_grad = own_grad + return_earlier(grad_window[reach - distance], distance)
    key_total = own_grad[:, :feat_width]
    value_total = own_grad[:, feat_width:]
    half_width = feat_width // 2
    grad_queries = query_full.astype(jnp.bfloat16)
    grad_keys = key_total.astype(jnp.bfloat16)
    grad_fresh = value_total[:, :half_width].astype(jnp.bfloat16)
    first_grad = value_total[:, half_width:]
    query_grad = jnp.dot(normed1.T, grad_queries, preferred_element_type=jnp.float32)
    key_grad = jnp.dot(normed1.T, grad_keys, preferred_element_type=jnp.float32)
    value_grad = jnp.dot(normed1.T, grad_fresh, preferred_element_type=jnp.float32)
    grad_normed1 = (
        jnp.dot(grad_queries, query_w.T, preferred_element_type=jnp.float32)
        + jnp.dot(grad_keys, key_w.T, preferred_element_type=jnp.float32)
        + jnp.dot(grad_fresh, value_w.T, preferred_element_type=jnp.float32)
    )
    grad_ln1, gain1_grad, shift1_grad = norm1_back(grad_normed1)
    input_grad = grad_resid + grad_ln1
    norm_grads = jnp.stack([gain1_grad, shift1_grad, gain2_grad, shift2_grad], axis=1)
    partial_list = (norm_grads, query_grad, key_grad, value_grad, out_grad, inner_grad, down_grad)
    rep_count = lax.axis_size("rep")
    pieces = (
        lax.psum_scatter(
            reorder_rows(norm_grads, fsdp_count, rep_count),
            ("rep", "fsdp"),
            scatter_dimension=0,
            tiled=True,
        ),
        lax.psum_scatter(
            reorder_rows(query_grad, fsdp_count, rep_count),
            ("rep", "fsdp"),
            scatter_dimension=0,
            tiled=True,
        ),
        lax.psum_scatter(
            reorder_rows(key_grad, fsdp_count, rep_count),
            ("rep", "fsdp"),
            scatter_dimension=0,
            tiled=True,
        ),
        lax.psum_scatter(
            reorder_rows(value_grad, fsdp_count, rep_count),
            ("rep", "fsdp"),
            scatter_dimension=0,
            tiled=True,
        ),
        lax.psum_scatter(
            reorder_rows(out_grad, fsdp_count, rep_count),
            ("rep", "fsdp"),
            scatter_dimension=0,
            tiled=True,
        ),
        lax.psum_scatter(
            reorder_rows(inner_grad, fsdp_count, rep_count),
            ("rep", "fsdp"),
            scatter_dimension=0,
            tiled=True,
        ),
        lax.psum_scatter(
            reorder_rows(down_grad, fsdp_count, rep_count),
            ("rep", "fsdp"),
            scatter_dimension=0,
            tiled=True,
        ),
    )
    spread = (
        lax.all_gather(pieces[0].astype(jnp.bfloat16), "rep", axis=0, tiled=True).astype(
            jnp.float32
        ),
        lax.all_gather(pieces[1].astype(jnp.bfloat16), "rep", axis=0, tiled=True).astype(
            jnp.float32
        ),
        lax.all_gather(pieces[2].astype(jnp.bfloat16), "rep", axis=0, tiled=True).astype(
            jnp.float32
        ),
        lax.all_gather(pieces[3].astype(jnp.bfloat16), "rep", axis=0, tiled=True).astype(
            jnp.float32
        ),
        lax.all_gather(pieces[4].astype(jnp.bfloat16), "rep", axis=0, tiled=True).astype(
            jnp.float32
        ),
        lax.all_gather(pieces[5].astype(jnp.bfloat16), "rep", axis=0, tiled=True).astype(
            jnp.float32
        ),
        lax.all_gather(pieces[6].astype(jnp.bfloat16), "rep", axis=0, tiled=True).astype(
            jnp.float32
        ),
    )
    summed = tuple(
        (
            piece_sum.reshape((whole.shape[0] // fsdp_count,) + whole.shape[1:])
            for piece_sum, whole in zip(spread, partial_list)
        )
    )
    norm_shard = summed[0]
    return (
        outputs,
        input_grad,
        first_grad,
        norm_shard[:, 0],
        norm_shard[:, 1],
        summed[1],
        summed[2],
        summed[3],
        summed[4],
        norm_shard[:, 2],
        norm_shard[:, 3],
        summed[5],
        summed[6],
    )


def solution(mesh):
    placed = (
        P(("rep", "fsdp"), None),
        P(("rep", "fsdp"), None),
        P(("rep", "fsdp"), None),
        P("rep"),
        P("rep"),
        P("rep", None, None),
        P("fsdp"),
        P("fsdp"),
        P("fsdp", None),
        P("fsdp", None),
        P("fsdp", None),
        P("fsdp", None),
        P("fsdp"),
        P("fsdp"),
        P("fsdp", None),
        P("fsdp", None),
    )
    return jax.shard_map(
        on_device,
        mesh=mesh,
        in_specs=placed,
        out_specs=(
            P(("rep", "fsdp"), None),
            P(("rep", "fsdp"), None),
            P(("rep", "fsdp"), None),
            P("fsdp"),
            P("fsdp"),
            P("fsdp", None),
            P("fsdp", None),
            P("fsdp", None),
            P("fsdp", None),
            P("fsdp"),
            P("fsdp"),
            P("fsdp", None),
            P("fsdp", None),
        ),
        check_vma=False,
    )
```

profile of v0, /device:TPU:0, one launch (start us, length us, event | category | flops | bytes accessed | tf_op | source)
XLA Modules:
  0.0 1321.9 jit_solution(18333137715302261885)
XLA Ops:
  13.4 14.0 %all-reduce.13 = (bf16[768]{0:T(1024)(128)(2,1)S(1)}, bf16[768]{0:T(1024)(128)(2,1)S(1)}, bf16[768]{0:T(1024)(128)(2,1)S(1)}, bf16[768]{0:T(1024)(128)(2,1)S(1)}) all-reduce(bf16[768]{0:T(1024)(128)(2,1)S(1)} %dynamic-update-slice.1, bf16[768]{0:T(1024)(128)(2,1)S(1)} %dynamic-update-slice, ...), channel_id=1, replica_groups=mesh['rep'=8,'fsdp'=4] {'fsdp'}, use_global_device_ids=true, to_apply=%add.1 | all-reduce | flops 3072 | bytes 12288
  28.0 23.2 %all_gather.54 = bf16[768,384]{1,0:T(8,128)(2,1)S(1)} all-gather(bf16[192,384]{1,0:T(8,128)(2,1)S(1)} %copy-done.27), channel_id=1, replica_groups=mesh['rep'=8,'fsdp'=4] {'fsdp'}, dimensions={0}, use_global_device_ids=true | all-gather | bytes 737280 | tf_op jit(solution)/shard_map/all_gather | solution.py:115
  61.4 8.4 gather_fusion
  70.5 8.4 gather_fusion.1
  85.4 13.9 %all-gather.10.cloned.1.call-done = bf16[768,768]{1,0:T(8,128)(2,1)} async-done(((bf16[192,768]{1,0:T(8,128)(2,1)}), bf16[768,768]{1,0:T(8,128)(2,1)}) %all-gather.10.cloned.1.call-update) | async-done | bytes 1179664 | tf_op jit(solution)/shard_map/all_gather | solution.py:113
  104.5 43.7 %collective-permute-done = bf16[768,1536]{0,1:T(8,128)(2,1)} collective-permute-done((bf16[768,1536]{0,1:T(8,128)(2,1)}, bf16[768,1536]{0,1:T(8,128)(2,1)}, u32[]{:S(2)}, u32[]{:S(2)}) %collective-permute-start) | collective-permute-done | bytes 2359328 | tf_op jit(solution)/shard_map/ppermute | solution.py:15
  148.2 11.2 maximum_maximum_fusion
  162.6 87.1 %while.38 = (s32[]{:T(128)}, bf16[768,768]{0,1:T(8,128)(2,1)S(1)}, f32[12,768]{1,0:T(8,128)}, bf16[1536,768]{0,1:T(8,128)(2,1)}, bf16[768,768]{0,1:T(8,128)(2,1)...) while((s32[]{:T(128)}, bf16[768,768]{0,1:T(8,128)(2,1)S(1)}, ...), condition=%wide.region_6.8_spmd.clone, body=%wide.region_3.7_spmd.clone.sunk | while | flops 644184576 | bytes 36703076 | solution.py:162
  256.1 8.6 fusion.62
  264.7 63.1 %all-gather.14.cloned.1.call-done = bf16[768,3072]{1,0:T(8,128)(2,1)} async-done(((bf16[192,3072]{1,0:T(8,128)(2,1)}), bf16[768,3072]{1,0:T(8,128)(2,1)}) %all-gather.14.cloned.1.call-update) | async-done | bytes 4718608 | tf_op jit(solution)/shard_map/all_gather | solution.py:175
  327.8 15.9 %fusion.18 = (bf16[768,3072]{1,0:T(8,128)(2,1)S(1)}, f32[768,3072]{1,0:T(8,128)}) fusion(f32[768,3072]{1,0:T(8,128)} %fusion.62, bf16[768,3072]{1,0:T(8,128)(2,1)} %all-gather.14.cloned.1.call-done, f32[768,768]{0,1:T(8,128)S(1)} %get-tuple-element.816, f32[768]{0:T(1024)} %convert_element_type.147, f32[768]{0:T(1024)} %convert_element_type.146, ...), kind=kOutput, calls=%fused_computation.43 | convolution fusion | flops 3674013696 | bytes 30683136 | tf_op jit(solution)/shard_map/dot_general | solution.py:182
  343.8 5.8 fusion.60
  368.5 270.2 %while.39 = (s32[]{:T(128)}, bf16[768,768]{0,1:T(8,128)(2,1)S(1)}, f32[1536,768]{1,0:T(8,128)}, f32[1536,768]{1,0:T(8,128)}, bf16[1536,768]{0,1:T(8,128)(2,1)}, ...) while((s32[]{:T(128)}, bf16[768,768]{0,1:T(8,128)(2,1)S(1)}, ...), condition=%wide.region_13.15_spmd.clone, body=%wide.region_11.14_spmd.clone.sunk | while | flops 1543371264 | bytes 86377304 | solution.py:238
  371.6 5.1 fusion.133
  382.0 8.3 multiply_reduce_fusion.6
  390.3 9.5 multiply_convert_fusion.5
  416.7 5.1 fusion.133
  427.0 8.3 multiply_reduce_fusion.6
  435.4 9.5 multiply_convert_fusion.5
  461.6 5.1 fusion.133
  472.0 8.3 multiply_reduce_fusion.6
  480.3 9.5 multiply_convert_fusion.5
  506.6 5.1 fusion.133
  517.0 8.3 multiply_reduce_fusion.6
  525.3 9.5 multiply_convert_fusion.5
  538.6 4.6 fusion.134
  551.6 5.1 fusion.133
  561.9 8.3 multiply_reduce_fusion.6
  570.3 9.5 multiply_convert_fusion.5
  596.5 5.1 fusion.133
  606.9 8.3 multiply_reduce_fusion.6
  615.2 9.5 multiply_convert_fusion.5
  665.0 8.8 fusion.47
  673.8 8.5 reshape.364
  682.3 13.4 %copy.158 = f32[4,8,73728]{2,0,1:T(4,128)} copy(f32[4,8,73728]{2,1,0:T(8,128)} %reshape.364) | data formatting | bytes 18874368 | tf_op jit(solution)/shard_map/reshape | solution.py:72
  695.7 8.7 copy.149
  704.4 13.0 fusion.49
  717.3 8.1 reshape.368
  725.5 13.4 %copy.157 = f32[4,8,73728]{2,0,1:T(4,128)} copy(f32[4,8,73728]{2,1,0:T(8,128)} %reshape.368) | data formatting | bytes 18874368 | tf_op jit(solution)/shard_map/reshape | solution.py:72
  738.9 8.8 copy.150
  748.8 6.1 fusion.56
  784.9 437.1 %all-reduce.15 = (bf16[3072]{0:T(1024)(128)(2,1)}, bf16[589824]{0:T(1024)(128)(2,1)}, bf16[589824]{0:T(1024)(128)(2,1)}, bf16[294912]{0:T(1024)(128)(2,1)}, bf16...) all-reduce(f32[3072]{0:T(1024)} %reshape.345, ...), channel_id=2, replica_groups=mesh['rep'=8,'fsdp'=4] {'rep','fsdp'}, use_global_device_ids=true, to_apply=%region_20.22.clone | all-reduce | flops 6786048 | bytes 40716288
  1227.1 10.8 add_convert_fusion
  1251.9 11.9 all-reduce.4
  1264.7 10.3 all_gather.62
  1276.9 8.3 all_gather.63
  1287.0 9.3 all_gather.64
  1297.9 8.3 all_gather.65
  (414 shorter events, 360.9 us)
Async XLA Ops:
  7.2 3.2 copy-start.17
  7.2 45.3 %all-gather.8.cloned.1.call-start = ((), (), s32[]{:S(2)}) async-start(), calls=%async_computation | async-start | bytes 1474560 | tf_op jit(solution)/shard_map/all_gather | solution.py:114
  7.9 91.3 %all-gather.10.cloned.1.call-start = ((), (), s32[]{:S(2)}) async-start(), calls=%async_computation.1 | async-start | bytes 1474560 | tf_op jit(solution)/shard_map/all_gather | solution.py:113
  8.7 241.1 %all-gather.12.cloned.1.call-start = ((), (), s32[]{:S(2)}) async-start(), calls=%async_computation.2 | async-start | bytes 1474560 | tf_op jit(solution)/shard_map/all_gather | solution.py:116
  9.4 3.2 copy-start.60
  9.5 3.4 copy-start.61
  9.5 3.7 copy-start.62
  9.5 246.6 %all-gather.16.cloned.1.call-start = ((), (), s32[]{:S(2)}) async-start(), calls=%async_computation.4 | async-start | bytes 5898240 | tf_op jit(solution)/shard_map/all_gather | solution.py:176
  10.0 317.8 %all-gather.14.cloned.1.call-start = ((), (), s32[]{:S(2)}) async-start(), calls=%async_computation.3 | async-start | bytes 5898240 | tf_op jit(solution)/shard_map/all_gather | solution.py:175
  10.4 17.6 %copy-start.27 = (bf16[192,384]{1,0:T(8,128)(2,1)S(1)}, bf16[192,384]{1,0:T(8,128)(2,1)}, u32[]{:S(2)}) copy-start(bf16[192,384]{1,0:T(8,128)(2,1)} %param.32) | copy-start | bytes 442372
  11.0 240.1 %copy-start.2 = (bf16[768,768]{0,1:T(8,128)(2,1)}, bf16[768,768]{0,1:T(8,128)(2,1)S(1)}, u32[]{:S(2)}) copy-start(bf16[768,768]{0,1:T(8,128)(2,1)S(1)} %copy.99) | copy-start | bytes 3538948
  27.4 71.9 %copy-start.51 = (f32[768]{0:T(1024)}, f32[768]{0:T(1024)S(1)}, u32[]{:S(2)}) copy-start(f32[768]{0:T(1024)S(1)} %convert_element_type.140) | copy-start | bytes 9220
  27.4 71.9 %copy-start.30 = (f32[768]{0:T(1024)}, f32[768]{0:T(1024)S(1)}, u32[]{:S(2)}) copy-start(f32[768]{0:T(1024)S(1)} %convert_element_type.139) | copy-start | bytes 9220
  27.6 71.6 %copy-start.28 = (f32[768]{0:T(1024)}, f32[768]{0:T(1024)S(1)}, u32[]{:S(2)}) copy-start(f32[768]{0:T(1024)S(1)} %broadcast_multiply_fusion.1) | copy-start | bytes 9220
  28.0 24.1 %copy-start.35 = (f32[768]{0:T(1024)}, f32[768]{0:T(1024)S(1)}, u32[]{:S(2)}) copy-start(f32[768]{0:T(1024)S(1)} %fusion.28) | copy-start | bytes 9220
  51.2 48.1 %copy-start.39 = (f32[768]{0:T(1024)}, f32[768]{0:T(1024)S(1)}, u32[]{:S(2)}) copy-start(f32[768]{0:T(1024)S(1)} %fusion.45) | copy-start | bytes 9220
  55.1 6.3 copy-start
  56.9 91.3 %collective-permute-start = (bf16[768,1536]{0,1:T(8,128)(2,1)}, bf16[768,1536]{0,1:T(8,128)(2,1)}, u32[]{:S(2)}, u32[]{:S(2)}) collective-permute-start(bf16[768,1536]{0,1:T(8,128)(2,1)} %pad_maximum_fusion), channel_id=1, source_target_pairs={{0,1},{1,2},{2,3},{4,5},{5,6},{6,7},{8,9},{9,10},{10,11},{12,13},{... | collective-permute-start | bytes 7077896 | tf_op jit(solution)/shard_map/ppermute | solution.py:15
  61.1 1247.1 %all-gather.18.cloned.1.call-start = ((), (), s32[]{:S(2)}) async-start(), calls=%async_computation.5 | async-start | bytes 1327104 | tf_op jit(solution)/shard_map/all_gather | solution.py:334
  61.4 9.1 copy-start.1
  70.5 8.4 copy-start.49
  187.4 3.1 copy-start.25
  253.9 102.2 %copy-start.4 = (f32[768,768]{0,1:T(8,128)}, f32[768,768]{0,1:T(8,128)S(1)}, u32[]{:S(2)}) copy-start(f32[768,768]{0,1:T(8,128)S(1)} %get-tuple-element.816) | copy-start | bytes 7077892
  327.8 15.9 %copy-start.55 = (bf16[768,3072]{1,0:T(8,128)(2,1)S(1)}, bf16[768,3072]{1,0:T(8,128)(2,1)}, u32[]{:S(2)}) copy-start(bf16[768,3072]{1,0:T(8,128)(2,1)} %all-gather.14.cloned.1.call-done) | copy-start | bytes 14155780
  343.7 5.9 copy-start.64
  349.6 3.3 copy-start.33
  349.6 3.3 copy-start.41
  349.6 3.3 copy-start.44
  352.9 3.2 copy-start.38
  353.0 3.2 copy-start.6
  638.7 12.8 copy-start.20
  638.7 4.2 copy-start.10
  643.6 3.7 copy-start.11
  647.3 3.6 copy-start.46
  647.3 4.2 copy-start.3
  647.3 4.2 copy-start.29
  647.3 4.2 copy-start.31
  647.3 4.2 copy-start.40
  647.3 4.2 copy-start.52
  649.0 99.8 %collective-permute-start.1 = (bf16[768,1536]{1,0:T(8,128)(2,1)}, bf16[768,1536]{1,0:T(8,128)(2,1)}, u32[]{:S(2)}, u32[]{:S(2)}) collective-permute-start(bf16[768,1536]{1,0:T(8,128)(2,1)} %slice.93), channel_id=1, source_target_pairs={{1,0},{2,1},{3,2},{5,4},{6,5},{7,6},{9,8},{10,9},{11,10},{13,12},{... | collective-permute-start | bytes 7077896 | tf_op jit(solution)/shard_map/ppermute | solution.py:15
  695.7 8.7 copy-start.19
  738.9 8.8 copy-start.21
  738.9 8.8 copy-start.57
  748.7 6.1 copy-start.53
  761.6 3.3 copy-start.47
  761.6 3.3 copy-start.48
  1223.6 87.7 %all-gather.20.cloned.1.call-start = ((), (), s32[]{:S(2)}) async-start(), calls=%async_computation.6 | async-start | bytes 1327104 | tf_op jit(solution)/shard_map/all_gather | solution.py:337
  1237.9 3.3 copy-start.8
  (36 other events, 78.3 us)
Sparse Core Ops, SparseCore 0:
  9.6 42.8 all-gather.7
  54.0 45.1 all-gather.9
  100.8 46.3 all-gather.11
  148.7 89.7 all-gather.15
  239.9 87.8 all-gather.13
  1223.7 22.1 all-gather.17
  1247.8 24.5 all-gather.19
where the time goes:
time: 1330 us; the launch traced here: 1320 us
  blocking collectives  522 us (39%)
  matrix products  271 us (20%)
  local copies, waits for them, and re-layouts  220 us (17%)
  other arithmetic  161 us (12%)
  waiting for transfers between devices  124 us (9%)
  between operations  16.8 us (1%)
    unnamed x3, blocking collectives  463 us
    reshape x14, local copies, waits for them, and re-layouts, reorder_rows(): grad_block.reshape(fsdp_count, rep_count, -1).transpose(1, 0, 2).reshape(-1)  63.8 us
    dot_general x12, matrix products, pair_scores(): jnp.einsum('qhd,khd->hqk', query_pair, key_pair, preferred_element_type=j...  63.7 us
    all_gather x1, waiting for transfers between devices, on_device(): lax.all_gather(w_in, 'fsdp', axis=0, tiled=True)  63.1 us
    unnamed x159, local copies, waits for them, and re-layouts  58.6 us
    convert_element_type x6, other arithmetic, backward_pair(): grad_scores = (probs * (grad_weights - inner_sum)).astype(jnp.bfloat16)  56.7 us
    ppermute x2, waiting for transfers between devices, shifted(): return lax.ppermute(block, axis, route)  43.7 us
    and x12, other arithmetic, visible_mask(): return inside[None, :] & same_tree & earlier & on_path  42.9 us
  transfers between devices with their start and end apart: 9, of which 4 were waited for; matrix products, arithmetic and copies ran while one was open for 22% of the time, Pallas kernels for 0%

commit v1 on v0

--- a/solution.py
+++ b/solution.py
@@ -7,6 +7,16 @@
 TREE_LEN = 1024
 epsilon = 1e-05
 far_below = -1e30
+
+
+def collect(x, axis, dim):
+    ways, here, step = (lax.axis_size(axis), lax.axis_index(axis), x.shape[dim])
+    lengths = [n * ways if d == dim else n for d, n in enumerate(x.shape)]
+    full = lax.dynamic_update_slice_in_dim(jnp.zeros(lengths, x.dtype), x, here * step, axis=dim)
+    for far in range(1, ways):
+        x = lax.ppermute(x, axis, [(d, (d + 1) % ways) for d in range(ways)])
+        full = lax.dynamic_update_slice_in_dim(full, x, (here - far) % ways * step, axis=dim)
+    return full
 
 
 def shifted(block, axis, distance):
@@ -172,7 +182,7 @@
     gain2, shift2, inner_w, down_w = (
         lax.all_gather(mlp_gain, "fsdp", axis=0, tiled=True),
         lax.all_gather(mlp_shift, "fsdp", axis=0, tiled=True),
-        lax.all_gather(w_in, "fsdp", axis=0, tiled=True),
+        collect(w_in, "fsdp", 0),
         lax.all_gather(w_down, "fsdp", axis=0, tiled=True),
     )
     normed2_f, norm2_back = jax.vjp(

time: 1330 us -> 1420 us (1.068)
  blocking collectives: 522 us -> 555 us
  waiting for transfers between devices: 124 us -> 154 us
  local copies, waits for them, and re-layouts: 220 us -> 238 us
    ppermute x0 -> x3, waiting for transfers between devices: none -> 152 us  [collect(): x = lax.ppermute(x, axis, [(d, (d + 1) % ways) for d in range(ways)])]
    all_gather x1 -> x0, waiting for transfers between devices: 63.1 us -> none  [on_device(): lax.all_gather(w_in, 'fsdp', axis=0, tiled=True)]
    ppermute x2, waiting for transfers between devices: 43.7 us -> 0.01 us  [shifted(): return lax.ppermute(block, axis, route)]
    unnamed x3, blocking collectives: 463 us -> 496 us
    unnamed x159 -> x181, local copies, waits for them, and re-layouts: 58.6 us -> 58.4 us
  transfers between devices with their start and end apart: 9 -> 11, of which waited for: 4 -> 2; matrix products, arithmetic and copies ran while one was open for 22% -> 21% of each run, Pallas kernels for 0% -> 0%
where the time goes in v1:
time: 1420 us; the launch traced here: 1410 us
  blocking collectives  555 us (39%)
  matrix products  270 us (19%)
  local copies, waits for them, and re-layouts  238 us (17%)
  other arithmetic  165 us (12%)
  waiting for transfers between devices  154 us (11%)
  between operations  16.8 us (1%)
    unnamed x3, blocking collectives  496 us
    ppermute x3, waiting for transfers between devices, collect(): x = lax.ppermute(x, axis, [(d, (d + 1) % ways) for d in range(ways)])  152 us
    reshape x14, local copies, waits for them, and re-layouts, reorder_rows(): grad_block.reshape(fsdp_count, rep_count, -1).transpose(1, 0, 2).reshape(-1)  63.8 us
    dot_general x12, matrix products, pair_scores(): jnp.einsum('qhd,khd->hqk', query_pair, key_pair, preferred_element_type=j...  63.5 us
    unnamed x181, local copies, waits for them, and re-layouts  58.4 us
    convert_element_type x6, other arithmetic, backward_pair(): grad_scores = (probs * (grad_weights - inner_sum)).astype(jnp.bfloat16)  56.7 us
    and x12, other arithmetic, visible_mask(): return inside[None, :] & same_tree & earlier & on_path  42.7 us
    dynamic_slice x42, local copies, waits for them, and re-layouts, pair_slice(): lax.dynamic_slice_in_dim(block, pair_index * 2 * HEAD, 2 * HEAD, 1)  31.6 us
  transfers between devices with their start and end apart: 11, of which 2 were waited for; matrix products, arithmetic and copies ran while one was open for 21% of the time, Pallas kernels for 0%

profile of v1, /device:TPU:0, one launch (start us, length us, event | category | flops | bytes accessed | tf_op | source)
XLA Modules:
  0.0 1412.4 jit_solution(8832658985549921708)
XLA Ops:
  14.6 11.7 gather_fusion
  26.4 11.7 gather_fusion.1
  40.6 22.9 %all-reduce.13 = (bf16[768]{0:T(1024)(128)(2,1)S(1)}, bf16[768]{0:T(1024)(128)(2,1)S(1)}, bf16[768]{0:T(1024)(128)(2,1)S(1)}, bf16[768]{0:T(1024)(128)(2,1)S(1)}) all-reduce(bf16[768]{0:T(1024)(128)(2,1)S(1)} %dynamic-update-slice.1, bf16[768]{0:T(1024)(128)(2,1)S(1)} %dynamic-update-slice, ...), channel_id=1, replica_groups=mesh['rep'=8,'fsdp'=4] {'fsdp'}, use_global_device_ids=true, to_apply=%add.1 | all-reduce | flops 3072 | bytes 12288
  68.8 23.2 %all_gather.51 = bf16[768,384]{1,0:T(8,128)(2,1)S(1)} all-gather(bf16[192,384]{1,0:T(8,128)(2,1)S(1)} %copy-done.29), channel_id=1, replica_groups=mesh['rep'=8,'fsdp'=4] {'fsdp'}, dimensions={0}, use_global_device_ids=true | all-gather | bytes 737280 | tf_op jit(solution)/shard_map/all_gather | solution.py:125
  97.4 4.9 collective-permute-start
  106.9 28.4 %collective-permute-done.2 = bf16[192,3072]{1,0:T(8,128)(2,1)} collective-permute-done((bf16[192,3072]{1,0:T(8,128)(2,1)}, bf16[192,3072]{1,0:T(8,128)(2,1)}, u32[]{:S(2)}, u32[]{:S(2)}) %collective-permute-start.2) | collective-permute-done | bytes 1179680 | tf_op jit(solution)/shard_map/ppermute | solution.py:17
  148.6 123.3 %collective-permute-done.3 = bf16[192,3072]{1,0:T(8,128)(2,1)} collective-permute-done((bf16[192,3072]{1,0:T(8,128)(2,1)}, bf16[192,3072]{1,0:T(8,128)(2,1)}, u32[]{:S(2)}, u32[]{:S(2)}) %collective-permute-start.3) | collective-permute-done | bytes 1179680 | tf_op jit(solution)/shard_map/ppermute | solution.py:17
  274.3 15.6 %maximum_maximum_fusion = bf16[1536,1536]{0,1:T(8,128)(2,1)S(1)} fusion(bf16[768,384]{0,1:T(8,128)(2,1)S(1)} %copy.100, bf16[768,384]{0,1:T(8,128)(2,1)S(1)} %convolution_convert_fusion.3, bf16[768,768]{0,1:T(8,128)(2,1)S(1)} %copy-done.15, bf16[768,1536]{0,1:T(8,128)(2,1)} %collective-permute-done), kind=kLoop, calls=%fused_computation.49 | loop fusion | flops 18874368 | bytes 9437184 | tf_op jit(solution)/shard_map/concatenate | solution.py:142
  293.1 87.0 %while.38 = (s32[]{:T(128)}, bf16[768,768]{0,1:T(8,128)(2,1)S(1)}, f32[12,768]{1,0:T(8,128)}, bf16[1536,768]{0,1:T(8,128)(2,1)}, bf16[768,768]{0,1:T(8,128)(2,1)...) while((s32[]{:T(128)}, bf16[768,768]{0,1:T(8,128)(2,1)S(1)}, ...), condition=%wide.region_6.8_spmd.clone, body=%wide.region_3.7_spmd.clone.sunk | while | flops 644184576 | bytes 36703076 | solution.py:172
  386.4 5.8 fusion.62
  392.2 14.4 %fusion.18 = (bf16[768,3072]{1,0:T(8,128)(2,1)S(1)}, f32[768,3072]{1,0:T(8,128)}) fusion(f32[768,3072]{1,0:T(8,128)S(1)} %fusion.62, bf16[768,3072]{1,0:T(8,128)(2,1)} %constant_dynamic-update-slice_fusion.6, f32[768,768]{0,1:T(8,128)S(1)} %get-tuple-element.816, f32[768]{0:T(1024)S(1)} %copy-done.65, f32[768]{0:T(1024)S(1)} %copy-done.47, ...), kind=kOutput, calls=%fused_computation.43 | convolution fusion | flops 3674013696 | bytes 30683136 | tf_op jit(solution)/shard_map/dot_general | solution.py:192
  406.7 9.9 fusion.60
  435.4 269.9 %while.39 = (s32[]{:T(128)}, bf16[768,768]{0,1:T(8,128)(2,1)S(1)}, f32[1536,768]{1,0:T(8,128)}, f32[1536,768]{1,0:T(8,128)}, bf16[1536,768]{0,1:T(8,128)(2,1)}, ...) while((s32[]{:T(128)}, bf16[768,768]{0,1:T(8,128)(2,1)S(1)}, ...), condition=%wide.region_13.15_spmd.clone, body=%wide.region_11.14_spmd.clone.sunk | while | flops 1543371264 | bytes 86377304 | solution.py:248
  438.6 5.1 fusion.133
  448.9 8.3 multiply_reduce_fusion.6
  457.2 9.5 multiply_convert_fusion.5
  483.6 5.1 fusion.133
  493.9 8.3 multiply_reduce_fusion.6
  502.2 9.5 multiply_convert_fusion.5
  515.6 4.6 fusion.134
  528.5 5.1 fusion.133
  538.8 8.3 multiply_reduce_fusion.6
  547.1 9.5 multiply_convert_fusion.5
  573.4 5.1 fusion.133
  583.7 8.3 multiply_reduce_fusion.6
  592.0 9.5 multiply_convert_fusion.5
  618.4 5.1 fusion.133
  628.7 8.3 multiply_reduce_fusion.6
  637.0 9.5 multiply_convert_fusion.5
  663.3 5.1 fusion.133
  673.6 8.3 multiply_reduce_fusion.6
  681.9 9.5 multiply_convert_fusion.5
  731.6 8.8 fusion.47
  740.5 8.5 reshape.364
  749.0 13.4 copy.158
  762.4 8.7 copy.149
  771.1 12.9 fusion.49
  784.0 8.2 reshape.368
  792.2 13.4 copy.157
  805.5 8.8 copy.150
  815.4 6.1 fusion.56
  851.6 460.8 %all-reduce.15 = (bf16[3072]{0:T(1024)(128)(2,1)}, bf16[589824]{0:T(1024)(128)(2,1)}, bf16[589824]{0:T(1024)(128)(2,1)}, bf16[294912]{0:T(1024)(128)(2,1)}, bf16...) all-reduce(f32[3072]{0:T(1024)} %reshape.345, ...), channel_id=2, replica_groups=mesh['rep'=8,'fsdp'=4] {'rep','fsdp'}, use_global_device_ids=true, to_apply=%region_20.22.clone | all-reduce | flops 6786048 | bytes 40716288
  1317.5 10.8 add_convert_fusion
  1342.3 11.9 all-reduce.4
  1355.2 10.5 all_gather.58
  1367.5 8.3 all_gather.59
  1377.5 9.4 all_gather.60
  1388.5 8.3 all_gather.61
  (444 shorter events, 372.2 us)
Async XLA Ops:
  7.2 5.5 copy-start.19
  7.2 85.8 %all-gather.7.cloned.1.call-start = ((), (), s32[]{:S(2)}) async-start(), calls=%async_computation | async-start | bytes 1474560 | tf_op jit(solution)/shard_map/all_gather | solution.py:124
  7.9 133.0 %all-gather.9.cloned.1.call-start = ((), (), s32[]{:S(2)}) async-start(), calls=%async_computation.1 | async-start | bytes 1474560 | tf_op jit(solution)/shard_map/all_gather | solution.py:123
  8.7 371.4 %all-gather.11.cloned.1.call-start = ((), (), s32[]{:S(2)}) async-start(), calls=%async_computation.2 | async-start | bytes 1474560 | tf_op jit(solution)/shard_map/all_gather | solution.py:126
  9.4 4.3 copy-start
  9.4 4.2 copy-start.1
  9.4 377.0 %all-gather.13.cloned.1.call-start = ((), (), s32[]{:S(2)}) async-start(), calls=%async_computation.3 | async-start | bytes 5898240 | tf_op jit(solution)/shard_map/all_gather | solution.py:186
  9.5 83.4 %collective-permute-start.1 = (bf16[192,3072]{1,0:T(8,128)(2,1)}, bf16[192,3072]{1,0:T(8,128)(2,1)}, u32[]{:S(2)}, u32[]{:S(2)}) collective-permute-start(bf16[192,3072]{1,0:T(8,128)(2,1)} %param.36), channel_id=1, source_target_pairs={{0,1},{1,2},{2,3},{3,0},{4,5},{5,6},{6,7},{7,4},{8,9},{9,10},{10,1... | collective-permute-start | bytes 3538952 | tf_op jit(solution)/shard_map/ppermute | solution.py:17
  12.6 1386.1 %all-gather.15.cloned.1.call-start = ((), (), s32[]{:S(2)}) async-start(), calls=%async_computation.4 | async-start | bytes 1327104 | tf_op jit(solution)/shard_map/all_gather | solution.py:344
  13.3 368.2 %copy-start.2 = (bf16[768,768]{0,1:T(8,128)(2,1)}, bf16[768,768]{0,1:T(8,128)(2,1)S(1)}, u32[]{:S(2)}) copy-start(bf16[768,768]{0,1:T(8,128)(2,1)S(1)} %copy.99) | copy-start | bytes 3538948
  26.3 11.8 copy-start.28
  26.3 12.1 copy-start.74
  26.3 13.3 copy-start.70
  26.3 13.6 copy-start.71
  26.3 13.8 copy-start.72
  26.3 14.0 copy-start.73
  38.1 30.7 %copy-start.29 = (bf16[192,384]{1,0:T(8,128)(2,1)S(1)}, bf16[192,384]{1,0:T(8,128)(2,1)}, u32[]{:S(2)}) copy-start(bf16[192,384]{1,0:T(8,128)(2,1)} %param.32) | copy-start | bytes 442372
  63.5 29.5 %copy-start.61 = (f32[768]{0:T(1024)}, f32[768]{0:T(1024)S(1)}, u32[]{:S(2)}) copy-start(f32[768]{0:T(1024)S(1)} %convert_element_type.140) | copy-start | bytes 9220
  63.5 29.5 %copy-start.33 = (f32[768]{0:T(1024)}, f32[768]{0:T(1024)S(1)}, u32[]{:S(2)}) copy-start(f32[768]{0:T(1024)S(1)} %convert_element_type.139) | copy-start | bytes 9220
  68.5 24.6 %copy-start.30 = (f32[768]{0:T(1024)}, f32[768]{0:T(1024)S(1)}, u32[]{:S(2)}) copy-start(f32[768]{0:T(1024)S(1)} %broadcast_multiply_fusion.1) | copy-start | bytes 9220
  68.8 24.0 %copy-start.40 = (f32[768]{0:T(1024)}, f32[768]{0:T(1024)S(1)}, u32[]{:S(2)}) copy-start(f32[768]{0:T(1024)S(1)} %fusion.28) | copy-start | bytes 9220
  92.9 42.4 %collective-permute-start.2 = (bf16[192,3072]{1,0:T(8,128)(2,1)}, bf16[192,3072]{1,0:T(8,128)(2,1)}, u32[]{:S(2)}, u32[]{:S(2)}) collective-permute-start(bf16[192,3072]{1,0:T(8,128)(2,1)} %collective-permute-done.1), channel_id=1, source_target_pairs={{0,1},{1,2},{2,3},{3,0},{4,5},{5,6},{6,7},{7,4},{8,9},{9,10},{10,1... | collective-permute-start | bytes 3538952 | tf_op jit(solution)/shard_map/ppermute | solution.py:17
  95.6 6.7 copy-start.55
  95.6 6.7 copy-start.54
  97.4 176.9 %collective-permute-start = (bf16[768,1536]{0,1:T(8,128)(2,1)}, bf16[768,1536]{0,1:T(8,128)(2,1)}, u32[]{:S(2)}, u32[]{:S(2)}) collective-permute-start(bf16[768,1536]{0,1:T(8,128)(2,1)} %pad_maximum_fusion), channel_id=1, source_target_pairs={{0,1},{1,2},{2,3},{4,5},{5,6},{6,7},{8,9},{9,10},{10,11},{12,13},{... | collective-permute-start | bytes 7077896 | tf_op jit(solution)/shard_map/ppermute | solution.py:25
  106.9 34.0 %copy-start.31 = (f32[768]{0:T(1024)S(1)}, f32[768]{0:T(1024)}, u32[]{:S(2)}) copy-start(f32[768]{0:T(1024)} %copy-done.30) | copy-start | bytes 9220
  106.9 34.0 %copy-start.34 = (f32[768]{0:T(1024)S(1)}, f32[768]{0:T(1024)}, u32[]{:S(2)}) copy-start(f32[768]{0:T(1024)} %copy-done.33) | copy-start | bytes 9220
  106.9 34.0 %copy-start.45 = (f32[768]{0:T(1024)S(1)}, f32[768]{0:T(1024)}, u32[]{:S(2)}) copy-start(f32[768]{0:T(1024)} %copy-done.44) | copy-start | bytes 9220
  106.9 34.0 %copy-start.62 = (f32[768]{0:T(1024)S(1)}, f32[768]{0:T(1024)}, u32[]{:S(2)}) copy-start(f32[768]{0:T(1024)} %copy-done.61) | copy-start | bytes 9220
  135.3 136.7 %collective-permute-start.3 = (bf16[192,3072]{1,0:T(8,128)(2,1)}, bf16[192,3072]{1,0:T(8,128)(2,1)}, u32[]{:S(2)}, u32[]{:S(2)}) collective-permute-start(bf16[192,3072]{1,0:T(8,128)(2,1)} %collective-permute-done.2), channel_id=1, source_target_pairs={{0,1},{1,2},{2,3},{3,0},{4,5},{5,6},{6,7},{7,4},{8,9},{9,10},{10,1... | collective-permute-start | bytes 3538952 | tf_op jit(solution)/shard_map/ppermute | solution.py:17
  146.1 128.2 %copy-start.15 = (bf16[768,768]{0,1:T(8,128)(2,1)S(1)}, bf16[768,768]{0,1:T(8,128)(2,1)}, u32[]{:S(2)}) copy-start(bf16[768,768]{0,1:T(8,128)(2,1)} %copy-done.14) | copy-start | bytes 3538948
  384.3 38.7 %copy-start.4 = (f32[768,768]{0,1:T(8,128)}, f32[768,768]{0,1:T(8,128)S(1)}, u32[]{:S(2)}) copy-start(f32[768,768]{0,1:T(8,128)S(1)} %get-tuple-element.816) | copy-start | bytes 7077892
  386.4 5.8 copy-start.37
  386.4 5.8 copy-start.47
  386.4 5.8 copy-start.51
  386.4 5.8 copy-start.65
  406.7 9.9 copy-start.75
  705.3 12.8 copy-start.22
  713.9 4.2 copy-start.3
  713.9 4.2 copy-start.32
  713.9 4.2 copy-start.35
  713.9 4.2 copy-start.46
  715.6 99.8 %collective-permute-start.4 = (bf16[768,1536]{1,0:T(8,128)(2,1)}, bf16[768,1536]{1,0:T(8,128)(2,1)}, u32[]{:S(2)}, u32[]{:S(2)}) collective-permute-start(bf16[768,1536]{1,0:T(8,128)(2,1)} %slice.93), channel_id=1, source_target_pairs={{1,0},{2,1},{3,2},{5,4},{6,5},{7,6},{9,8},{10,9},{11,10},{13,12},{... | collective-permute-start | bytes 7077896 | tf_op jit(solution)/shard_map/ppermute | solution.py:25
  762.4 8.7 copy-start.21
  805.5 8.8 copy-start.23
  805.5 8.8 copy-start.68
  815.4 6.1 copy-start.64
  1314.0 87.7 %all-gather.17.cloned.1.call-start = ((), (), s32[]{:S(2)}) async-start(), calls=%async_computation.5 | async-start | bytes 1327104 | tf_op jit(solution)/shard_map/all_gather | solution.py:347
  (49 other events, 123.2 us)
Sparse Core Ops, SparseCore 0:
  9.6 50.8 all-gather.6
  62.1 40.1 all-gather.8
  103.9 47.9 all-gather.10
  153.3 139.4 all-gather.12
  1314.1 22.3 all-gather.14
  1338.3 24.5 all-gather.16
